TPU v7x, 512 devices: a whole 4x4x16 slice. The times are simulated.
512 devices in a mesh: ctx: 64 (over y, z_lo, core), exp: 8 (over z_hi, x).
Axes of the slice: x: 4, y: 4, z: 16 (z_hi: 2, z_lo: 8; z = z_hi * 8 + z_lo), core: 2. Of those that a mesh axis runs over, the one named last changes fastest.
Arguments:
- queries: bfloat16 [8192, 32, 128], P('ctx', 'exp'), may hold values from -100 to 100
- keys: bfloat16 [8192, 2, 128], P('ctx'), may hold values from -4 to 4
- values: bfloat16 [8192, 2, 128], P('ctx'), may hold values from -4 to 4
- resid: bfloat16 [8192, 4096], P('ctx', 'exp'), may hold values from -20 to 20
- gain: float32 [4096], P('exp'), may hold values from 0.1 to 1.9
- expert_ids: int32 [8192, 8], P('ctx'), may hold values from 0 to 127, all different within a row; in each aligned block of 128 rows (0 to 127, 128 to 255, ...) at most 10 rows name the same one
- gate_scores: float32 [8192, 8], P('ctx'), may hold values from 0.05 to 1
- w_gate_up: bfloat16 [64, 4096, 2, 768], P('ctx', 'exp'), may hold values from -0.09375 to 0.09375
- w_down: bfloat16 [64, 768, 4096], P('ctx', None, 'exp'), may hold values from -0.625 to 0.625
- w_out: bfloat16 [32, 128, 4096], P('exp', 'ctx'), may hold values from -0.5 to 0.5
Outputs:
- context: bfloat16 [8192, 32, 128], P('ctx', 'exp')
- mixed: bfloat16 [8192, 4096], P('ctx', 'exp')
Inputs may be any that keep to these rules, and one draw needn't show every extreme that they name: `expert_ids`: each row names 8 different experts; within the 128 rows of one index of ctx no expert is named more than 10 times.
All inputs are finite; a program needn't handle non-finite values.
Results may differ from a plain program's by a relative error of at most 0.02.
Values may be sent and summed in bfloat16 or wider, within the bound.
No kernel may reach another device: no remote copies, remote signals or barrier semaphores. Data moves between devices by JAX's collectives and lax.ppermute only.
A program may use at most 64 MiB of HBM per device.

v0:
```python
import math
import jax
import jax.numpy as jnp
from jax import lax
from jax.sharding import PartitionSpec as P

D = 4096
HQ = 32
KVH = 2
EXPERTS = 128
TOPK = 8
masked_score = -1e30
epsilon = 1e-06


def attend_piece(state_now, pair_piece, offset, query_rows, query_pos, last_pos, scaling):
    key_piece, value_piece = pair_piece
    length = key_piece.shape[0]

    def compute(state_in):
        running, denominator, numerator = state_in
        scores = (
            jnp.einsum("rd,kd->rk", query_rows, key_piece, preferred_element_type=jnp.float32)
            * scaling
        )
        key_pos = jnp.arange(length, dtype=jnp.int32)
        visible = key_pos[None, :] <= query_pos[:, None]
        masked = jnp.where(visible, scores, masked_score)
        highest = jnp.maximum(running, jnp.max(masked, axis=1))
        weights_exp = jnp.where(visible, jnp.exp(masked - highest[:, None]), 0.0)
        rounded = weights_exp.astype(jnp.bfloat16)
        numerator = jnp.dot(rounded, value_piece, preferred_element_type=jnp.float32)
        denominator = jnp.sum(weights_exp, axis=1)
        return (highest, denominator, numerator)

    def untouched(state_in):
        return state_in

    return lax.cond(offset <= last_pos, compute, untouched, state_now)


def body(queries, keys, values, resid, gain, expert_ids, gate_scores, w_gate_up, w_down, w_out):
    tokens_here = queries.shape[0]
    heads_here = queries.shape[1]
    head_size = queries.shape[2]
    ctx_count = lax.axis_size("ctx")
    ctx_place = lax.axis_index("ctx")
    exp_place = lax.axis_index("exp")
    own_pos = ctx_place * tokens_here + jnp.arange(tokens_here, dtype=jnp.int32)
    query_sets = (queries, own_pos)
    group_index = exp_place * heads_here // (HQ // KVH)
    key_local = lax.dynamic_index_in_dim(keys, group_index, 1, keepdims=False)
    value_local = lax.dynamic_index_in_dim(values, group_index, 1, keepdims=False)
    scaling = 1.0 / math.sqrt(head_size)
    set_queries, set_pos = query_sets
    set_rows = set_queries.shape[0] * heads_here
    initial = [
        (
            jnp.full((set_rows,), masked_score, jnp.float32),
            jnp.zeros((set_rows,), jnp.float32),
            jnp.zeros((set_rows, head_size), jnp.float32),
        )
    ]
    rows_set = set_queries.reshape(set_rows, head_size)
    pos_set = jnp.repeat(set_pos, heads_here)
    last_set = jnp.max(set_pos)
    updated = [
        attend_piece(
            tuple(initial)[0],
            (
                lax.all_gather(key_local, "ctx", axis=0, tiled=True),
                lax.all_gather(value_local, "ctx", axis=0, tiled=True),
            ),
            jnp.int32(0),
            rows_set,
            pos_set,
            last_set,
            scaling,
        )
    ]
    folded = tuple(updated)
    pieces_out = []
    for state_set in folded:
        normalized = state_set[2] / state_set[1][:, None]
        pieces_out.append(normalized.reshape(-1, heads_here, head_size).astype(jnp.bfloat16))
    context = pieces_out[0]
    whole_out = lax.all_gather(w_out, "ctx", axis=1, tiled=True)
    projected = jnp.einsum("thp,hpd->td", context, whole_out, preferred_element_type=jnp.float32)
    attended = lax.psum_scatter(
        projected.astype(jnp.bfloat16), "exp", scatter_dimension=1, tiled=True
    ).astype(jnp.float32)
    hidden_state = resid.astype(jnp.float32) + attended
    square_sum = lax.psum(jnp.sum(hidden_state * hidden_state, axis=1), "exp")
    inverse = lax.rsqrt(square_sum / D + epsilon)
    normed = (hidden_state * inverse[:, None] * gain[None, :]).astype(jnp.bfloat16)
    capacity = max(2, 5 * tokens_here * TOPK // (4 * EXPERTS))
    flat_ids = expert_ids.reshape(-1)
    onehot = (flat_ids[:, None] == jnp.arange(ctx_count, dtype=jnp.int32)[None, :]).astype(
        jnp.int32
    )
    earlier = jnp.cumsum(onehot, axis=0) - onehot
    rank_of = jnp.sum(earlier * onehot, axis=1)
    active = flat_ids < ctx_count
    slot_of = jnp.where(active, flat_ids * capacity + rank_of, -1).reshape(tokens_here, TOPK)
    slot_range = jnp.arange(ctx_count * capacity, dtype=jnp.int32)
    dispatch_map = jnp.zeros((ctx_count * capacity, tokens_here), jnp.bfloat16)
    for column in range(TOPK):
        dispatch_map = dispatch_map + (slot_range[:, None] == slot_of[None, :, column]).astype(
            jnp.bfloat16
        )
    local_width = normed.shape[1]
    outgoing = jnp.dot(dispatch_map, normed, preferred_element_type=jnp.float32).astype(
        jnp.bfloat16
    )
    outgoing = outgoing.reshape(ctx_count, capacity, local_width)
    arrived = lax.all_to_all(outgoing, "ctx", split_axis=0, concat_axis=0, tiled=True)
    sources = arrived.shape[0]
    width_slots = arrived.shape[1]
    row_block = arrived.reshape(sources * width_slots, local_width)
    partial_sum = jnp.einsum(
        "rd,dgf->rgf", row_block, w_gate_up[0], preferred_element_type=jnp.float32
    )
    summed = lax.psum(partial_sum.astype(jnp.bfloat16), "exp").astype(jnp.float32)
    hidden_units = (jax.nn.silu(summed[:, 0]) * summed[:, 1]).astype(jnp.bfloat16)
    result = jnp.dot(hidden_units, w_down[0], preferred_element_type=jnp.float32).astype(
        jnp.bfloat16
    )
    result = result.reshape(sources, width_slots, local_width)
    returned = lax.all_to_all(result, "ctx", split_axis=0, concat_axis=0, tiled=True)
    back_rows = returned.reshape(ctx_count * capacity, local_width)
    picked = jnp.take(back_rows, jnp.maximum(slot_of, 0).reshape(-1), axis=0).reshape(
        tokens_here, TOPK, local_width
    )
    weight_now = gate_scores / jnp.sum(gate_scores, axis=1, keepdims=True)
    weight_now = jnp.where(active.reshape(tokens_here, TOPK), weight_now, 0.0)
    routed = jnp.zeros((tokens_here, local_width), jnp.float32)
    for column in range(TOPK):
        routed = routed + weight_now[:, column : column + 1] * picked[:, column].astype(jnp.float32)
    mixed = (hidden_state + routed).astype(jnp.bfloat16)
    return (context, mixed)


def solution(mesh):
    in_specs = (
        P("ctx", "exp", None),
        P("ctx", None, None),
        P("ctx", None, None),
        P("ctx", "exp"),
        P("exp"),
        P("ctx", None),
        P("ctx", None),
        P("ctx", "exp", None, None),
        P("ctx", None, "exp"),
        P("exp", "ctx", None),
    )
    out_specs = (P("ctx", "exp", None), P("ctx", "exp"))
    return jax.shard_map(body, mesh=mesh, in_specs=in_specs, out_specs=out_specs, check_vma=False)
```

profile of v0, /device:TPU:7, one launch (start us, length us, event | category | flops | bytes accessed | tf_op | source)
XLA Modules:
  0.0 899.9 jit_solution(3959203209659631209)
XLA Ops:
  7.2 1.0 constant_dynamic-slice_fusion.1
  8.3 0.6 copy.83
  9.0 0.9 constant_dynamic-slice_fusion
  9.9 0.6 copy.84
  10.6 1.5 copy.72
  12.2 0.6 fusion.63
  13.4 122.9 %all-gather.8.cloned.1.call-done = bf16[8192,1,128]{2,0,1:T(8,128)(2,1)} async-done(((bf16[128,1,128]{2,0,1:T(8,128)(2,1)}), bf16[8192,1,128]{2,0,1:T(8,128)(2,1)}) %all-gather.8.cloned.1.call-update) | async-done | bytes 2097168 | tf_op jit(solution)/shard_map/all_gather | solution.py:71
  136.3 118.7 %all-gather.10.cloned.1.call-done = bf16[8192,1,128]{2,0,1:T(8,128)(2,1)} async-done(((bf16[128,1,128]{2,0,1:T(8,128)(2,1)}), bf16[8192,1,128]{2,0,1:T(8,128)(2,1)}) %all-gather.10.cloned.1.call-update) | async-done | bytes 2097168 | tf_op jit(solution)/shard_map/all_gather | solution.py:72
  255.0 16.5 %conditional.1 = (f32[512]{0:T(512)S(1)}, f32[512,128]{1,0:T(8,128)S(1)}) conditional(s32[]{:T(128)} %convert_element_type.124, () %tuple.16, (s32[128]{0:T(128)S(1)}, bf16[128,4,128]{2,1,0:T(4,128)(2,1)}, bf16[8192,128]{1,0:T(8,128)(2,1)}, bf16[8192,128]{1,0:T(8,128)(2,1)}) %tuple.48), branch_computations={%region_1.2_spmd, %region_2.5_spmd} | conditional | flops 2214592000 | bytes 63332908 | solution.py:39
  255.0 0.1 broadcast_in_dim.27
  255.1 0.1 le.24
  255.2 5.0 fusion
  260.2 5.8 fusion.3
  266.0 5.5 fusion.2
  271.5 0.1 divide_convert_fusion
  271.7 104.7 %all-gather.6.cloned.1.call-done = bf16[4,128,4096]{2,0,1:T(4,128)(2,1)} async-done(((bf16[4,2,4096]{2,0,1:T(4,128)(2,1)}), bf16[4,128,4096]{2,0,1:T(4,128)(2,1)}) %all-gather.6.cloned.1.call-update) | async-done | bytes 4194320 | tf_op jit(solution)/shard_map/all_gather | solution.py:87
  376.3 8.0 fusion.8
  384.4 0.2 all-reduce.2.cloned.1.call-start
  384.6 0.1 copy.75
  384.7 0.1 eq.149
  384.8 0.1 eq.145
  384.9 18.0 %reduce-window.6 = s32[64,8,128]{2,1,0:T(8,128)S(1)} reduce-window(s32[64,8,128]{2,1,0:T(8,128)S(1)} %fusion.35, s32[]{:T(128)} %constant.71.clone.1), window={size=1x1x128 pad=0_0x0_0x127_0}, to_apply=%region_7.8 | reduce-window | flops 8323072 | bytes 524292 | tf_op jit(solution)/shard_map/reduce-window
  402.9 0.1 slice.114
  403.1 0.1 copy.77
  403.3 0.1 copy.78
  403.3 0.1 broadcast_add_fusion
  403.6 0.1 reduce_sum.40
  403.7 92.3 %reduce-scatter.2.cloned.1.call-done = bf16[128,512]{1,0:T(8,128)(2,1)} async-done(((bf16[128,4096]{1,0:T(8,128)(2,1)}), bf16[128,512]{1,0:T(8,128)(2,1)}) %reduce-scatter.2.cloned.1.call-update) | async-done | bytes 131088 | tf_op jit(solution)/shard_map/reduce_scatter | solution.py:89
  496.0 1.0 multiply_reduce_fusion
  497.1 29.7 %psum.14 = f32[128]{0:T(128)S(1)} all-reduce(f32[128]{0:T(128)S(1)} %multiply_reduce_fusion), channel_id=1, replica_groups=mesh['ctx'=64,'exp'=8] {'exp'}, use_global_device_ids=true, to_apply=%region_11.12 | all-reduce | flops 128 | bytes 1024 | tf_op jit(solution)/shard_map/psum | solution.py:93
  526.7 1.4 convolution_convert_fusion.1
  528.1 0.2 reshape.120
  528.3 62.0 %all_to_all.10 = bf16[64,10,512]{2,1,0:T(8,128)(2,1)} all-to-all(bf16[64,10,512]{2,1,0:T(8,128)(2,1)S(1)} %reshape.120), channel_id=1, replica_groups=mesh['ctx'=64,'exp'=8] {'ctx'}, dimensions={0} | all-to-all | bytes 1310720 | tf_op jit(solution)/shard_map/all_to_all | solution.py:116
  590.3 1.4 reshape.144
  591.7 2.5 convolution_convert_fusion
  594.2 228.4 %all-reduce.2.cloned.1.call-done = bf16[640,2,768]{2,0,1:T(8,128)(2,1)} async-done(((bf16[640,2,768]{2,0,1:T(8,128)(2,1)}), bf16[640,2,768]{2,0,1:T(8,128)(2,1)}) %all-reduce.2.cloned.1.call-update) | async-done | bytes 1966096 | tf_op jit(solution)/shard_map/psum | solution.py:123
  822.5 1.8 convert_element_type.143
  824.4 0.7 convolution_convert_fusion.2
  825.1 1.2 reshape.122
  826.3 9.2 %all-to-all-start.1 = ((bf16[64,10,512]{2,1,0:T(8,128)(2,1)}), bf16[64,10,512]{2,1,0:T(8,128)(2,1)S(1)}, u32[]{:S(2)}, u32[]{:S(2)}) async-start(bf16[64,10,512]{2,1,0:T(8,128)(2,1)} %reshape.122), calls=%async_computation.2 | async-start | bytes 2097152 | tf_op jit(solution)/shard_map/all_to_all | solution.py:129
  835.5 0.1 copy.81
  835.6 0.1 reshape.124
  835.8 0.6 slice_bitcast_fusion.23
  836.4 50.4 %all-to-all-done.1 = bf16[64,10,512]{2,1,0:T(8,128)(2,1)S(1)} async-done(((bf16[64,10,512]{2,1,0:T(8,128)(2,1)}), bf16[64,10,512]{2,1,0:T(8,128)(2,1)S(1)}, u32[]{:S(2)}, u32[]{:S(2)}) %all-to-all-start.1) | async-done | bytes 655392 | tf_op jit(solution)/shard_map/all_to_all | solution.py:129
  886.9 0.2 reshape.123
  887.1 4.0 gather_fusion
  891.1 0.7 copy_select_fusion
  891.8 1.6 fusion.28
  (42 shorter events, 0.6 us)
Async XLA Ops:
  7.2 584.5 %copy-start = (bf16[1,512,2,768]{3,2,1,0:T(2,128)(2,1)S(1)}, bf16[1,512,2,768]{3,2,1,0:T(2,128)(2,1)}, u32[]{:S(2)}) copy-start(bf16[1,512,2,768]{3,2,1,0:T(2,128)(2,1)} %param.19) | copy-start | bytes 4718596
  7.2 129.1 %all-gather.8.cloned.1.call-start = ((), (), s32[]{:S(2)}) async-start(), calls=%async_computation.6 | async-start | bytes 2129920 | tf_op jit(solution)/shard_map/all_gather | solution.py:71
  8.9 246.1 %all-gather.10.cloned.1.call-start = ((), (), s32[]{:S(2)}) async-start(), calls=%async_computation.7 | async-start | bytes 2129920 | tf_op jit(solution)/shard_map/all_gather | solution.py:72
  10.5 365.8 %all-gather.6.cloned.1.call-start = ((), (), s32[]{:S(2)}) async-start(), calls=%async_computation.3 | async-start | bytes 4259840 | tf_op jit(solution)/shard_map/all_gather | solution.py:87
  12.1 483.9 %reduce-scatter.2.cloned.1.call-start = ((), (), s32[]{:S(2)}) async-start(), calls=%async_computation.4 | async-start | bytes 1179648 | tf_op jit(solution)/shard_map/reduce_scatter | solution.py:89
  255.2 5.0 copy-start.6
  271.5 113.1 %copy-start.4 = (s32[128,8]{0,1:T(8,128)S(1)}, s32[128,8]{0,1:T(8,128)}, u32[]{:S(2)}) copy-start(s32[128,8]{0,1:T(8,128)} %param.17) | copy-start | bytes 12292
  271.7 113.2 %copy-start.3 = (bf16[512,128]{1,0:T(8,128)(2,1)}, bf16[512,128]{1,0:T(8,128)(2,1)S(1)}, u32[]{:S(2)}) copy-start(bf16[512,128]{1,0:T(8,128)(2,1)S(1)} %divide_convert_fusion) | copy-start | bytes 393220
  376.3 119.7 %copy-start.1 = (bf16[128,512]{1,0:T(8,128)(2,1)S(1)}, bf16[128,512]{1,0:T(8,128)(2,1)}, u32[]{:S(2)}) copy-start(bf16[128,512]{1,0:T(8,128)(2,1)} %param.15) | copy-start | bytes 393220
  376.3 150.4 %copy-start.8 = (f32[512]{0:T(512)S(1)}, f32[512]{0:T(512)}, u32[]{:S(2)}) copy-start(f32[512]{0:T(512)} %param.16) | copy-start | bytes 6148
  384.4 438.2 %all-reduce.2.cloned.1.call-start = ((), (), s32[]{:S(2)}) async-start(), calls=%async_computation.5 | async-start | bytes 3932160 | tf_op jit(solution)/shard_map/psum | solution.py:123
  594.2 230.2 %copy-start.7 = (bf16[1,768,512]{2,1,0:T(8,128)(2,1)S(1)}, bf16[1,768,512]{2,1,0:T(8,128)(2,1)}, u32[]{:S(2)}) copy-start(bf16[1,768,512]{2,1,0:T(8,128)(2,1)} %param.20) | copy-start | bytes 2359300
  824.4 11.3 %copy-start.5 = (f32[128,8]{0,1:T(8,128)S(1)}, f32[128,8]{0,1:T(8,128)}, u32[]{:S(2)}) copy-start(f32[128,8]{0,1:T(8,128)} %param.18) | copy-start | bytes 12292
  826.3 60.5 %all-to-all-start.1 = ((bf16[64,10,512]{2,1,0:T(8,128)(2,1)}), bf16[64,10,512]{2,1,0:T(8,128)(2,1)S(1)}, u32[]{:S(2)}, u32[]{:S(2)}) async-start(bf16[64,10,512]{2,1,0:T(8,128)(2,1)} %reshape.122), calls=%async_computation.2 | async-start | bytes 2097152 | tf_op jit(solution)/shard_map/all_to_all | solution.py:129
  887.1 4.7 copy-start.2
Sparse Core Ops, SparseCore 0:
  10.7 125.5 all-gather.7
  138.4 116.4 all-gather.9
  257.7 118.5 all-gather.5
  384.5 111.4 reduce-scatter.1
  594.3 228.1 all-reduce.1
where the time goes:
time: 900 us
  waiting for transfers between devices  717 us (80%)
  blocking collectives  91.6 us (10%)
  other arithmetic  29.8 us (3%)
  matrix products  23.4 us (3%)
  between operations  14.7 us (2%)
  local copies, waits for them, and re-layouts  13.5 us (2%)
  starting transfers between devices  9.59 us (1%)
    psum x1, waiting for transfers between devices, body(): lax.psum(partial_sum.astype(jnp.bfloat16), 'exp').astype(jnp.float32)  228 us
    all_gather x1, waiting for transfers between devices, body(): lax.all_gather(key_local, 'ctx', axis=0, tiled=True)  123 us
    all_gather x1, waiting for transfers between devices, body(): lax.all_gather(value_local, 'ctx', axis=0, tiled=True)  119 us
    all_gather x1, waiting for transfers between devices, body(): whole_out = lax.all_gather(w_out, 'ctx', axis=1, tiled=True)  105 us
    reduce_scatter x1, waiting for transfers between devices, body(): lax.psum_scatter(projected.astype(jnp.bfloat16), 'exp', scatter_dimension...  92.3 us
    all_to_all x1, blocking collectives, body(): lax.all_to_all(outgoing, 'ctx', split_axis=0, concat_axis=0, tiled=True)  62 us
    all_to_all x1, waiting for transfers between devices, body(): lax.all_to_all(result, 'ctx', split_axis=0, concat_axis=0, tiled=True)  50.4 us
    psum x1, blocking collectives, body(): square_sum = lax.psum(jnp.sum(hidden_state * hidden_state, axis=1), 'exp')  29.7 us
  transfers between devices with their start and end apart: 6, of which 6 were waited for; matrix products, arithmetic and copies ran while one was open for 4% of the time, Pallas kernels for 0%

commit v1 on v0

--- a/solution.py
+++ b/solution.py
@@ -120,7 +120,13 @@
     partial_sum = jnp.einsum(
         "rd,dgf->rgf", row_block, w_gate_up[0], preferred_element_type=jnp.float32
     )
-    summed = lax.psum(partial_sum.astype(jnp.bfloat16), "exp").astype(jnp.float32)
+
+    def apply_shifts_all(in_array, peer_axis):
+        p_next = lax.all_gather(in_array, peer_axis)
+        current_arr = jnp.sum(p_next, 0)
+        return current_arr
+
+    summed = apply_shifts_all(partial_sum.astype(jnp.bfloat16), "exp").astype(jnp.float32)
     hidden_units = (jax.nn.silu(summed[:, 0]) * summed[:, 1]).astype(jnp.bfloat16)
     result = jnp.dot(hidden_units, w_down[0], preferred_element_type=jnp.float32).astype(
         jnp.bfloat16

time: 900 us -> 1200 us (1.33)
  waiting for transfers between devices: 717 us -> 982 us
  starting transfers between devices: 9.59 us -> 30.9 us
    all_gather x0 -> x1, waiting for transfers between devices: none -> 493 us  [apply_shifts_all(): p_next = lax.all_gather(in_array, peer_axis)]
    psum x1 -> x0, waiting for transfers between devices: 228 us -> none  [body(): lax.psum(partial_sum.astype(jnp.bfloat16), 'exp').astype(jnp.float32)]
    all_to_all x1, starting transfers between devices: 9.2 us -> 30.5 us  [body(): lax.all_to_all(result, 'ctx', split_axis=0, concat_axis=0, tiled=True)]
  transfers between devices with their start and end apart: 6 -> 6, of which waited for: 6 -> 6; matrix products, arithmetic and copies ran while one was open for 4% -> 3% of each run, Pallas kernels for 0% -> 0%
where the time goes in v1:
time: 1200 us; the launch traced here: 1190 us
  waiting for transfers between devices  982 us (82%)
  blocking collectives  91.6 us (8%)
  other arithmetic  37 us (3%)
  starting transfers between devices  30.9 us (3%)
  matrix products  23.3 us (2%)
  between operations  14.7 us (1%)
  local copies, waits for them, and re-layouts  14.3 us (1%)
    all_gather x1, waiting for transfers between devices, apply_shifts_all(): p_next = lax.all_gather(in_array, peer_axis)  493 us
    all_gather x1, waiting for transfers between devices, body(): lax.all_gather(key_local, 'ctx', axis=0, tiled=True)  123 us
    all_gather x1, waiting for transfers between devices, body(): lax.all_gather(value_local, 'ctx', axis=0, tiled=True)  119 us
    all_gather x1, waiting for transfers between devices, body(): whole_out = lax.all_gather(w_out, 'ctx', axis=1, tiled=True)  105 us
    reduce_scatter x1, waiting for transfers between devices, body(): lax.psum_scatter(projected.astype(jnp.bfloat16), 'exp', scatter_dimension...  92.3 us
    all_to_all x1, blocking collectives, body(): lax.all_to_all(outgoing, 'ctx', split_axis=0, concat_axis=0, tiled=True)  62 us
    all_to_all x1, waiting for transfers between devices, body(): lax.all_to_all(result, 'ctx', split_axis=0, concat_axis=0, tiled=True)  50.4 us
    all_to_all x1, starting transfers between devices, body(): lax.all_to_all(result, 'ctx', split_axis=0, concat_axis=0, tiled=True)  30.5 us
  transfers between devices with their start and end apart: 6, of which 6 were waited for; matrix products, arithmetic and copies ran while one was open for 3% of the time, Pallas kernels for 0%

profile of v1, /device:TPU:7, one launch (start us, length us, event | category | flops | bytes accessed | tf_op | source)
XLA Modules:
  0.0 1193.7 jit_solution(16482536256510242516)
XLA Ops:
  7.2 1.0 constant_dynamic-slice_fusion.1
  8.3 0.6 copy.83
  9.0 0.9 constant_dynamic-slice_fusion
  9.9 0.6 copy.84
  10.6 1.5 copy.72
  12.2 0.6 fusion.63
  13.5 122.8 %all-gather.10.cloned.1.call-done = bf16[8192,1,128]{2,0,1:T(8,128)(2,1)} async-done(((bf16[128,1,128]{2,0,1:T(8,128)(2,1)}), bf16[8192,1,128]{2,0,1:T(8,128)(2,1)}) %all-gather.10.cloned.1.call-update) | async-done | bytes 2097168 | tf_op jit(solution)/shard_map/all_gather | solution.py:71
  136.3 118.7 %all-gather.12.cloned.1.call-done = bf16[8192,1,128]{2,0,1:T(8,128)(2,1)} async-done(((bf16[128,1,128]{2,0,1:T(8,128)(2,1)}), bf16[8192,1,128]{2,0,1:T(8,128)(2,1)}) %all-gather.12.cloned.1.call-update) | async-done | bytes 2097168 | tf_op jit(solution)/shard_map/all_gather | solution.py:72
  255.0 16.5 %conditional.1 = (f32[512]{0:T(512)S(1)}, f32[512,128]{1,0:T(8,128)S(1)}) conditional(s32[]{:T(128)} %convert_element_type.126, () %tuple.16, (s32[128]{0:T(128)S(1)}, bf16[128,4,128]{2,1,0:T(4,128)(2,1)}, bf16[8192,128]{1,0:T(8,128)(2,1)}, bf16[8192,128]{1,0:T(8,128)(2,1)}) %tuple.48), branch_computations={%region_1.2_spmd, %region_2.5_spmd} | conditional | flops 2214592000 | bytes 63332908 | solution.py:39
  255.1 0.1 le.24
  255.2 5.0 fusion
  260.2 5.8 fusion.3
  266.0 5.5 fusion.2
  271.5 0.1 divide_convert_fusion
  271.7 104.7 %all-gather.8.cloned.1.call-done = bf16[4,128,4096]{2,0,1:T(4,128)(2,1)} async-done(((bf16[4,2,4096]{2,0,1:T(4,128)(2,1)}), bf16[4,128,4096]{2,0,1:T(4,128)(2,1)}) %all-gather.8.cloned.1.call-update) | async-done | bytes 4194320 | tf_op jit(solution)/shard_map/all_gather | solution.py:87
  376.3 8.0 fusion.8
  384.4 0.2 all-gather.14.cloned.1.call-start
  384.6 0.1 copy.75
  384.7 0.1 eq.149
  384.8 0.1 eq.145
  384.9 18.0 %reduce-window.6 = s32[64,8,128]{2,1,0:T(8,128)S(1)} reduce-window(s32[64,8,128]{2,1,0:T(8,128)S(1)} %fusion.35, s32[]{:T(128)} %constant.72.clone.1), window={size=1x1x128 pad=0_0x0_0x127_0}, to_apply=%region_7.8 | reduce-window | flops 8323072 | bytes 524292 | tf_op jit(solution)/shard_map/reduce-window
  402.9 0.1 slice.114
  403.1 0.1 copy.77
  403.3 0.1 copy.78
  403.3 0.1 broadcast_add_fusion
  403.7 92.3 %reduce-scatter.2.cloned.1.call-done = bf16[128,512]{1,0:T(8,128)(2,1)} async-done(((bf16[128,4096]{1,0:T(8,128)(2,1)}), bf16[128,512]{1,0:T(8,128)(2,1)}) %reduce-scatter.2.cloned.1.call-update) | async-done | bytes 131088 | tf_op jit(solution)/shard_map/reduce_scatter | solution.py:89
  496.0 1.0 multiply_reduce_fusion
  497.1 29.7 %psum.7 = f32[128]{0:T(128)S(1)} all-reduce(f32[128]{0:T(128)S(1)} %multiply_reduce_fusion), channel_id=1, replica_groups=mesh['ctx'=64,'exp'=8] {'exp'}, use_global_device_ids=true, to_apply=%region_11.12 | all-reduce | flops 128 | bytes 1024 | tf_op jit(solution)/shard_map/psum | solution.py:93
  526.7 1.4 convolution_convert_fusion.1
  528.1 0.2 reshape.120
  528.3 62.0 %all_to_all.10 = bf16[64,10,512]{2,1,0:T(8,128)(2,1)} all-to-all(bf16[64,10,512]{2,1,0:T(8,128)(2,1)S(1)} %reshape.120), channel_id=1, replica_groups=mesh['ctx'=64,'exp'=8] {'ctx'}, dimensions={0} | all-to-all | bytes 1310720 | tf_op jit(solution)/shard_map/all_to_all | solution.py:116
  590.3 1.4 reshape.145
  591.7 2.5 convolution_convert_fusion
  594.2 492.8 %all-gather.14.cloned.1.call-done = bf16[5120,2,768]{2,0,1:T(8,128)(2,1)} async-done(((bf16[640,2,768]{2,0,1:T(8,128)(2,1)}), bf16[5120,2,768]{2,0,1:T(8,128)(2,1)}) %all-gather.14.cloned.1.call-update) | async-done | bytes 15728656 | tf_op jit(solution)/shard_map/all_gather | solution.py:125
  1086.9 8.8 reduce_sum.54
  1095.7 0.3 convert_element_type.145
  1096.0 0.8 copy-done.8
  1096.9 0.7 convolution_convert_fusion.2
  1097.6 1.2 reshape.122
  1098.8 30.5 %all-to-all-start.1 = ((bf16[64,10,512]{2,1,0:T(8,128)(2,1)}), bf16[64,10,512]{2,1,0:T(8,128)(2,1)S(1)}, u32[]{:S(2)}, u32[]{:S(2)}) async-start(bf16[64,10,512]{2,1,0:T(8,128)(2,1)} %reshape.122), calls=%async_computation.2 | async-start | bytes 2097152 | tf_op jit(solution)/shard_map/all_to_all | solution.py:135
  1129.3 0.1 copy.81
  1129.4 0.1 reshape.124
  1129.6 0.6 slice_bitcast_fusion.23
  1130.2 50.4 %all-to-all-done.1 = bf16[64,10,512]{2,1,0:T(8,128)(2,1)S(1)} async-done(((bf16[64,10,512]{2,1,0:T(8,128)(2,1)}), bf16[64,10,512]{2,1,0:T(8,128)(2,1)S(1)}, u32[]{:S(2)}, u32[]{:S(2)}) %all-to-all-start.1) | async-done | bytes 655392 | tf_op jit(solution)/shard_map/all_to_all | solution.py:135
  1180.6 0.2 reshape.123
  1180.9 4.0 gather_fusion
  1184.9 0.7 copy_select_fusion
  1185.6 1.6 fusion.28
  (45 shorter events, 0.7 us)
Async XLA Ops:
  7.2 584.5 %copy-start = (bf16[1,512,2,768]{3,2,1,0:T(2,128)(2,1)S(1)}, bf16[1,512,2,768]{3,2,1,0:T(2,128)(2,1)}, u32[]{:S(2)}) copy-start(bf16[1,512,2,768]{3,2,1,0:T(2,128)(2,1)} %param.19) | copy-start | bytes 4718596
  7.2 129.1 %all-gather.10.cloned.1.call-start = ((), (), s32[]{:S(2)}) async-start(), calls=%async_computation.5 | async-start | bytes 2129920 | tf_op jit(solution)/shard_map/all_gather | solution.py:71
  8.9 246.1 %all-gather.12.cloned.1.call-start = ((), (), s32[]{:S(2)}) async-start(), calls=%async_computation.6 | async-start | bytes 2129920 | tf_op jit(solution)/shard_map/all_gather | solution.py:72
  10.5 365.8 %all-gather.8.cloned.1.call-start = ((), (), s32[]{:S(2)}) async-start(), calls=%async_computation.3 | async-start | bytes 4259840 | tf_op jit(solution)/shard_map/all_gather | solution.py:87
  12.1 483.9 %reduce-scatter.2.cloned.1.call-start = ((), (), s32[]{:S(2)}) async-start(), calls=%async_computation.4 | async-start | bytes 1179648 | tf_op jit(solution)/shard_map/reduce_scatter | solution.py:89
  255.2 5.0 copy-start.7
  271.5 113.1 %copy-start.5 = (s32[128,8]{0,1:T(8,128)S(1)}, s32[128,8]{0,1:T(8,128)}, u32[]{:S(2)}) copy-start(s32[128,8]{0,1:T(8,128)} %param.17) | copy-start | bytes 12292
  271.7 113.2 %copy-start.4 = (bf16[512,128]{1,0:T(8,128)(2,1)}, bf16[512,128]{1,0:T(8,128)(2,1)S(1)}, u32[]{:S(2)}) copy-start(bf16[512,128]{1,0:T(8,128)(2,1)S(1)} %divide_convert_fusion) | copy-start | bytes 393220
  376.3 119.7 %copy-start.1 = (bf16[128,512]{1,0:T(8,128)(2,1)S(1)}, bf16[128,512]{1,0:T(8,128)(2,1)}, u32[]{:S(2)}) copy-start(bf16[128,512]{1,0:T(8,128)(2,1)} %param.15) | copy-start | bytes 393220
  376.3 150.4 %copy-start.9 = (f32[512]{0:T(512)S(1)}, f32[512]{0:T(512)}, u32[]{:S(2)}) copy-start(f32[512]{0:T(512)} %param.16) | copy-start | bytes 6148
  384.4 702.6 %all-gather.14.cloned.1.call-start = ((), (), s32[]{:S(2)}) async-start(), calls=%async_computation.7 | async-start | bytes 17694720 | tf_op jit(solution)/shard_map/all_gather | solution.py:125
  1095.7 1.1 copy-start.8
  1096.9 32.7 %copy-start.6 = (f32[128,8]{0,1:T(8,128)S(1)}, f32[128,8]{0,1:T(8,128)}, u32[]{:S(2)}) copy-start(f32[128,8]{0,1:T(8,128)} %param.18) | copy-start | bytes 12292
  1098.8 81.9 %all-to-all-start.1 = ((bf16[64,10,512]{2,1,0:T(8,128)(2,1)}), bf16[64,10,512]{2,1,0:T(8,128)(2,1)S(1)}, u32[]{:S(2)}, u32[]{:S(2)}) async-start(bf16[64,10,512]{2,1,0:T(8,128)(2,1)} %reshape.122), calls=%async_computation.2 | async-start | bytes 2097152 | tf_op jit(solution)/shard_map/all_to_all | solution.py:135
  1180.9 4.7 copy-start.2
  1180.9 4.7 copy-start.3
Sparse Core Ops, SparseCore 0:
  10.7 125.5 all-gather.9
  138.4 116.4 all-gather.11
  257.7 118.5 all-gather.7
  384.5 111.4 reduce-scatter.1
  594.3 492.5 all-gather.13
